TPU v7x, 128 devices: a whole 4x4x4 slice. The times are simulated.
128 devices in a mesh: grp: 8 (over z, core), mem: 16 (over y, x).
Axes of the slice: x: 4, y: 4, z: 4, core: 2. Of those that a mesh axis runs over, the one named last changes fastest.
Arguments:
- forcing: float32 [3, 1024, 4096], P(None, ('grp', 'mem')), may hold values from -6 to 6
- viscosity: float32 [1024, 4096], P(('grp', 'mem')), may hold values from 0.1 to 10
- refinement: int32 [1024], P(('grp', 'mem')), may hold values from 0 to 1
- face_owner: int32 [4096, 1], P(('grp', 'mem')), may hold values from 0 to 15; in each aligned block of 32 rows (0 to 31, 32 to 63, ...) at most 4 rows name the same one
- face_block: int32 [1024, 4], P(('grp', 'mem')), may hold values from 0 to 7
- plane_block: int32 [1024, 2], P(('grp', 'mem')), may hold values from 0 to 7
- hanging: int32 [1024, 6], P(('grp', 'mem')), may hold values 0 or 1
- coarse_solver: float32 [8, 384, 384], P('grp', 'mem'), may hold values from -0.3125 to 0.3125
Outputs:
- velocity: float32 [3, 1024, 4096], P(None, ('grp', 'mem'))
- residual: float32 [3, 1024, 4096], P(None, ('grp', 'mem'))
Inputs may be any that keep to these rules, and one draw needn't show every extreme that they name: `face_owner`: among the 32 rows of one device no member appears more than 4 times, and some member appears exactly 4 times.
All inputs are finite; a program needn't handle non-finite values. No bound on the sum of `hanging` on one device may be relied on, other than what follows from the above.
Results may differ from a plain program's by a relative error of at most 0.0001.
Values sent between devices are 32-bit elements; how exact they have to be, the bound alone decides.
A program may use at most 64 MiB of HBM per device.

v0:
```python
import math

import jax
import jax.numpy as jnp
from jax import lax
from jax.sharding import PartitionSpec as P

EDGE = 16
DEG = 3
CELLS = 4096
FACE = 256


MASS_TERM = 1.0
LOWER_BOUND = 0.25
UPPER_BOUND = 2.0
HIGHEST = lax.Precision.HIGHEST


def shifted_2(block, axis, distance):
    devices = range(lax.axis_size(axis))
    route = [(i - distance, i) for i in devices if i - distance in devices]
    return lax.ppermute(block, axis, route)


def coarsen(plane_vals):
    leading = plane_vals.shape[:-1]
    squares = plane_vals.reshape(leading + (EDGE // 2, 2, EDGE // 2, 2))
    average = jnp.mean(squares, axis=(-3, -1), keepdims=True)
    return jnp.broadcast_to(average, squares.shape).reshape(leading + (FACE,))


def tables():
    lanes = jnp.arange(FACE, dtype=jnp.int32)
    lane_k = lanes % EDGE
    lane_j = lanes // EDGE
    sources = [lanes - 1, lanes + 1, lanes - EDGE, lanes + EDGE]
    valid = [lane_k > 0, lane_k < EDGE - 1, lane_j > 0, lane_j < EDGE - 1]
    shift_mat = jnp.concatenate(
        [
            ((lanes[:, None] == sources[d][None, :]) & valid[d][None, :]).astype(jnp.float32)
            for d in range(4)
        ],
        axis=1,
    )
    places = jnp.arange(EDGE, dtype=jnp.int32)
    picks = [places * EDGE, places * EDGE + EDGE - 1, places, (EDGE - 1) * EDGE + places]
    pick_mats = [(lanes[:, None] == picks[d][None, :]).astype(jnp.float32) for d in range(4)]
    return (shift_mat, pick_mats)


def far_faces(upper_planes, lower_planes, plane_block):
    arrived = []
    for by_step, outgoing in ((1, upper_planes), (-1, lower_planes)):
        arrived.append(shifted_2(outgoing, "grp", by_step))
    lower_ghost = jnp.take(arrived[0], plane_block[:, 0], axis=1)
    upper_ghost = jnp.take(arrived[1], plane_block[:, 1], axis=1)
    return (lower_ghost, upper_ghost)


def local(
    forcing, viscosity, refinement, face_owner, face_block, plane_block, hanging, coarse_solver
):
    blocks_here = forcing.shape[1]
    shift_mat, pick_mats = tables()
    pick_all = jnp.concatenate(pick_mats, axis=1)
    forcing_cube = forcing.reshape(3, blocks_here, EDGE, FACE)
    effective = (
        viscosity.reshape(blocks_here, EDGE, FACE)
        * jnp.exp2(-refinement.astype(jnp.float32))[:, None, None]
    )
    owners = face_owner[:, 0]
    opposite = jnp.array([1, 0, 3, 2], jnp.int32)
    wanted = (face_block * 4 + opposite[None, :]).reshape(-1)

    def near_faces(face_rows):
        gathered = lax.all_gather(face_rows, "mem", axis=0, tiled=True)
        return gathered[owners * (4 * blocks_here) + wanted]

    def ghost_set(stacked):
        channels = stacked.shape[0]
        picked = jnp.einsum("cbil,lm->cbim", stacked, pick_all, precision=HIGHEST)
        face_rows = (
            picked.reshape(channels, blocks_here, EDGE, 4, EDGE)
            .transpose(1, 3, 0, 2, 4)
            .reshape(blocks_here * 4, channels * FACE)
        )
        ghost_rows = near_faces(face_rows).reshape(blocks_here, 4, channels, FACE)
        result = [ghost_rows[:, direction].transpose(1, 0, 2) for direction in range(4)]
        lower_ghost, upper_ghost = far_faces(
            stacked[:, :, EDGE - 1, :], stacked[:, :, 0, :], plane_block
        )
        result.append(lower_ghost)
        result.append(upper_ghost)
        return [
            jnp.where(
                hanging[:, direction][None, :, None] == 1,
                coarsen(result[direction]),
                result[direction],
            )
            for direction in range(6)
        ]

    def beside(values, ghosts):
        channels = values.shape[0]
        shifted = jnp.einsum("cbil,lm->cbim", values, shift_mat, precision=HIGHEST)
        nearby = []
        for direction in range(4):
            placed = jnp.einsum(
                "cbim,lm->cbil",
                ghosts[direction].reshape(channels, blocks_here, EDGE, EDGE),
                pick_mats[direction],
                precision=HIGHEST,
            )
            nearby.append(shifted[..., direction * FACE : (direction + 1) * FACE] + placed)
        nearby.append(jnp.concatenate([ghosts[4][:, :, None, :], values[:, :, :-1, :]], axis=2))
        nearby.append(jnp.concatenate([values[:, :, 1:, :], ghosts[5][:, :, None, :]], axis=2))
        return nearby

    nearby_eff = beside(effective[None], ghost_set(effective[None]))
    weights = [0.5 * (effective + nearby_eff[direction][0]) for direction in range(6)]
    diagonal = MASS_TERM * effective
    for direction in range(6):
        diagonal = diagonal + weights[direction]

    def operate(values):
        nearby = beside(values, ghost_set(values))
        applied = diagonal * values
        for direction in range(6):
            applied = applied - weights[direction] * nearby[direction]
        return applied

    midpoint = 0.5 * (UPPER_BOUND + LOWER_BOUND)
    half_width = 0.5 * (UPPER_BOUND - LOWER_BOUND)
    sigma_ratio = midpoint / half_width

    def smooth(solution, residual):
        rho_now = 1.0 / sigma_ratio
        step_dir = residual / (diagonal * midpoint)
        for sweep_index in range(DEG):
            solution = solution + step_dir
            residual = residual - operate(step_dir)
            if sweep_index < DEG - 1:
                rho_next = 1.0 / (2.0 * sigma_ratio - rho_now)
                step_dir = rho_next * rho_now * step_dir + 2.0 * rho_next / half_width * (
                    residual / diagonal
                )
                rho_now = rho_next
        return (solution, residual)

    solution, residual = smooth(jnp.zeros_like(forcing_cube), forcing_cube)
    coarse_local = (jnp.sum(residual, axis=(2, 3)) / math.sqrt(CELLS)).T.reshape(-1)
    rows_here = coarse_solver[0]
    correction = jnp.dot(
        rows_here,
        lax.all_gather(coarse_local, "mem", axis=0, tiled=True),
        precision=HIGHEST,
        preferred_element_type=jnp.float32,
    )
    lifted = jnp.broadcast_to(
        correction.reshape(blocks_here, 3).T[:, :, None, None], forcing_cube.shape
    )
    solution = solution + lifted
    residual = residual - operate(lifted)
    solution, residual = smooth(solution, residual)
    return (solution.reshape(forcing.shape), residual.reshape(forcing.shape))


def solution(mesh):
    in_specs = (
        P(None, ("grp", "mem"), None),
        P(("grp", "mem"), None),
        P(("grp", "mem")),
        P(("grp", "mem"), None),
        P(("grp", "mem"), None),
        P(("grp", "mem"), None),
        P(("grp", "mem"), None),
        P("grp", "mem", None),
    )
    out_specs = (P(None, ("grp", "mem"), None), P(None, ("grp", "mem"), None))
    return jax.shard_map(local, mesh=mesh, in_specs=in_specs, out_specs=out_specs, check_vma=False)
```

profile of v0, /device:TPU:0, one launch (start us, length us, event | category | flops | bytes accessed | tf_op | source)
XLA Modules:
  0.0 607.3 jit_solution(15840290535157774675)
XLA Ops:
  14.4 24.8 %all_gather.27 = f32[512,256]{1,0:T(8,128)S(1)} all-gather(f32[32,256]{1,0:T(8,128)S(1)} %reshape.1007), channel_id=1, replica_groups=mesh['grp'=8,'mem'=16] {'mem'}, dimensions={0}, use_global_device_ids=true | all-gather | bytes 557056 | tf_op jit(solution)/shard_map/all_gather | solution.py:77
  71.7 24.8 %all-gather.8.cloned.1.call-done = f32[512,768]{1,0:T(8,128)} async-done(((f32[32,768]{1,0:T(8,128)}), f32[512,768]{1,0:T(8,128)}) %all-gather.8.cloned.1.call-update) | async-done | bytes 1572880 | tf_op jit(solution)/shard_map/all_gather | solution.py:77
  96.5 2.2 gather_fusion.1
  129.4 2.1 gather_fusion.12
  134.5 2.0 reduce_sum.457
  138.3 1.7 copy.571
  142.9 2.0 gather_fusion.13
  148.0 1.9 reduce_sum.458
  151.7 1.7 copy.576
  154.9 11.5 %all-gather.10.cloned.1.call-done = f32[512,768]{1,0:T(8,128)} async-done(((f32[32,768]{1,0:T(8,128)}), f32[512,768]{1,0:T(8,128)}) %all-gather.10.cloned.1.call-update) | async-done | bytes 1572880 | tf_op jit(solution)/shard_map/all_gather | solution.py:77
  166.4 2.8 gather_fusion.2
  172.3 1.7 copy.553
  174.0 2.0 reduce_sum.453
  177.7 1.8 copy.554
  179.5 1.7 copy.557
  181.1 2.0 reduce_sum.454
  184.9 1.8 copy.558
  186.6 1.7 copy.561
  188.3 2.0 reduce_sum.455
  192.0 1.8 copy.562
  193.8 1.7 copy.565
  195.5 1.9 reduce_sum.456
  199.2 1.8 copy.566
  226.1 2.0 fusion.97
  229.0 1.7 collective-permute-start.7
  236.2 28.4 %all-gather.12.cloned.1.call-done = f32[512,768]{1,0:T(8,128)} async-done(((f32[32,768]{1,0:T(8,128)}), f32[512,768]{1,0:T(8,128)}) %all-gather.12.cloned.1.call-update) | async-done | bytes 1572880 | tf_op jit(solution)/shard_map/all_gather | solution.py:77
  264.5 2.2 gather_fusion.3
  281.1 38.1 %all-reduce = f32[384]{0:T(512)S(1)} all-reduce(f32[384]{0:T(512)S(1)} %dynamic-update-slice), channel_id=1, replica_groups=mesh['grp'=8,'mem'=16] {'mem'}, use_global_device_ids=true, to_apply=%add | all-reduce | flops 384 | bytes 3072
  321.0 2.1 reshape.1069
  324.6 2.0 fusion.95
  333.9 29.4 %all-gather.14.cloned.1.call-done = f32[512,768]{1,0:T(8,128)} async-done(((f32[32,768]{1,0:T(8,128)}), f32[512,768]{1,0:T(8,128)}) %all-gather.14.cloned.1.call-update) | async-done | bytes 1572880 | tf_op jit(solution)/shard_map/all_gather | solution.py:77
  363.2 2.2 gather_fusion.4
  380.8 2.0 fusion.93
  401.3 21.2 %all-gather.16.cloned.1.call-done = f32[512,768]{1,0:T(8,128)} async-done(((f32[32,768]{1,0:T(8,128)}), f32[512,768]{1,0:T(8,128)}) %all-gather.16.cloned.1.call-update) | async-done | bytes 1572880 | tf_op jit(solution)/shard_map/all_gather | solution.py:77
  422.5 2.2 gather_fusion.5
  450.0 2.1 copy.658
  452.1 2.1 reshape.1107
  455.6 2.0 fusion.91
  476.4 21.0 %all-gather.18.cloned.1.call-done = f32[512,768]{1,0:T(8,128)} async-done(((f32[32,768]{1,0:T(8,128)}), f32[512,768]{1,0:T(8,128)}) %all-gather.18.cloned.1.call-update) | async-done | bytes 1572880 | tf_op jit(solution)/shard_map/all_gather | solution.py:77
  497.3 2.2 gather_fusion.6
  526.1 1.9 collective-permute-start.14
  531.8 1.8 reshape.1125
  546.6 22.0 %all-gather.20.cloned.1.call-done = f32[512,768]{1,0:T(8,128)} async-done(((f32[32,768]{1,0:T(8,128)}), f32[512,768]{1,0:T(8,128)}) %all-gather.20.cloned.1.call-update) | async-done | bytes 1572880 | tf_op jit(solution)/shard_map/all_gather | solution.py:77
  568.5 2.2 gather_fusion.7
  575.7 1.7 copy.691
  579.6 1.8 copy.692
  585.3 1.8 copy.696
  590.9 1.8 copy.700
  (852 shorter events, 291.5 us)
Async XLA Ops:
  7.2 32.1 %copy-start.144 = (s32[4]{0:T(128)S(1)}, s32[4]{0:T(128)}, u32[]{:S(2)}) copy-start(s32[4]{0:T(128)} %constant.145.clone) | copy-start | bytes 52
  7.2 32.1 %copy-start.142 = (s32[8,4]{0,1:T(4,128)S(1)}, s32[8,4]{0,1:T(4,128)}, u32[]{:S(2)}) copy-start(s32[8,4]{0,1:T(4,128)} %param.17) | copy-start | bytes 388
  7.2 32.3 %copy-start.145 = (s32[32,1]{0,1:T(1,128)S(1)}, s32[32,1]{0,1:T(1,128)}, u32[]{:S(2)}) copy-start(s32[32,1]{0,1:T(1,128)} %param.16) | copy-start | bytes 388
  7.2 89.3 %all-gather.8.cloned.1.call-start = ((), (), s32[]{:S(2)}) async-start(), calls=%async_computation | async-start | bytes 1671168 | tf_op jit(solution)/shard_map/all_gather | solution.py:77
  7.9 39.2 %copy-start.140 = (f32[8]{0:T(128)}, f32[8]{0:T(128)S(1)}, u32[]{:S(2)}) copy-start(f32[8]{0:T(128)S(1)} %multiply_exponential_fusion) | copy-start | bytes 100
  8.9 35.8 %collective-permute-start = (f32[1,8,256]{2,0,1:T(1,128)S(1)}, f32[1,8,256]{2,0,1:T(1,128)S(1)}, u32[]{:S(2)}, u32[]{:S(2)}) collective-permute-start(f32[1,8,256]{2,0,1:T(1,128)S(1)} %get-tuple-element.104), channel_id=1, source_target_pairs={{0,16},{16,32},{32,48},{48,64},{64,80},{80,96},{96,112},{1,17},{17... | collective-permute-start | bytes 24584 | tf_op jit(solution)/shard_map/ppermute | solution.py:23
  10.2 35.6 %collective-permute-start.1 = (f32[1,8,256]{2,0,1:T(1,128)S(1)}, f32[1,8,256]{2,0,1:T(1,128)S(1)}, u32[]{:S(2)}, u32[]{:S(2)}) collective-permute-start(f32[1,8,256]{2,0,1:T(1,128)S(1)} %get-tuple-element.105), channel_id=1, source_target_pairs={{16,0},{32,16},{48,32},{64,48},{80,64},{96,80},{112,96},{17,1},{33... | collective-permute-start | bytes 24584 | tf_op jit(solution)/shard_map/ppermute | solution.py:23
  11.5 32.2 %copy-start.129 = (s32[16]{0:T(128)}, s32[16]{0:T(128)S(1)}, u32[]{:S(2)}) copy-start(s32[16]{0:T(128)S(1)} %iota_add_fusion.4) | copy-start | bytes 196
  11.5 31.4 %copy-start.122 = (s32[16]{0:T(128)}, s32[16]{0:T(128)S(1)}, u32[]{:S(2)}) copy-start(s32[16]{0:T(128)S(1)} %broadcast_add_fusion) | copy-start | bytes 196
  11.6 31.1 %copy-start.127 = (s32[16]{0:T(128)}, s32[16]{0:T(128)S(1)}, u32[]{:S(2)}) copy-start(s32[16]{0:T(128)S(1)} %iota_multiply_fusion) | copy-start | bytes 196
  11.6 29.4 %copy-start.70 = (s32[8,6]{1,0:T(8,128)S(1)}, s32[8,6]{1,0:T(8,128)}, u32[]{:S(2)}) copy-start(s32[8,6]{1,0:T(8,128)} %param.19) | copy-start | bytes 580
  41.4 5.6 copy-start.118
  49.7 116.8 %all-gather.10.cloned.1.call-start = ((), (), s32[]{:S(2)}) async-start(), calls=%async_computation.1 | async-start | bytes 1671168 | tf_op jit(solution)/shard_map/all_gather | solution.py:77
  49.9 5.5 collective-permute-start.2
  51.9 11.4 %collective-permute-start.3 = (f32[3,8,256]{2,1,0:T(8,128)}, f32[3,8,256]{2,1,0:T(8,128)}, u32[]{:S(2)}, u32[]{:S(2)}) collective-permute-start(f32[3,8,256]{2,1,0:T(8,128)} %bitcast.760), channel_id=1, source_target_pairs={{16,0},{32,16},{48,32},{64,48},{80,64},{96,80},{112,96},{17,1},{33... | collective-permute-start | bytes 73736 | tf_op jit(solution)/shard_map/ppermute | solution.py:23
  123.3 141.2 %all-gather.12.cloned.1.call-start = ((), (), s32[]{:S(2)}) async-start(), calls=%async_computation.2 | async-start | bytes 1671168 | tf_op jit(solution)/shard_map/all_gather | solution.py:77
  123.4 5.3 collective-permute-start.4
  125.6 89.6 %copy-start.1 = (f32[3,8,16,1024]{3,2,1,0:T(8,128)}, f32[3,8,16,1024]{3,2,1,0:T(8,128)S(1)}, u32[]{:S(2)}) copy-start(f32[3,8,16,1024]{3,2,1,0:T(8,128)S(1)} %fusion.99) | copy-start | bytes 4718596
  127.2 14.3 %collective-permute-start.5 = (f32[3,8,256]{2,1,0:T(8,128)}, f32[3,8,256]{2,1,0:T(8,128)}, u32[]{:S(2)}, u32[]{:S(2)}) collective-permute-start(f32[3,8,256]{2,1,0:T(8,128)} %bitcast.758), channel_id=1, source_target_pairs={{16,0},{32,16},{48,32},{64,48},{80,64},{96,80},{112,96},{17,1},{33... | collective-permute-start | bytes 73736 | tf_op jit(solution)/shard_map/ppermute | solution.py:23
  221.4 141.8 %all-gather.14.cloned.1.call-start = ((), (), s32[]{:S(2)}) async-start(), calls=%async_computation.3 | async-start | bytes 1671168 | tf_op jit(solution)/shard_map/all_gather | solution.py:77
  224.8 6.7 %copy-start.72 = (pred[8]{0:T(512)(128)(4,1)S(1)}, pred[8]{0:T(512)(128)(4,1)}, u32[]{:S(2)}) copy-start(pred[8]{0:T(512)(128)(4,1)} %copy-done.71) | copy-start | bytes 28
  224.8 6.0 collective-permute-start.6
  229.0 5.6 copy-start.78
  229.0 4.9 collective-permute-start.7
  279.4 39.8 %copy-start.69 = (f32[8,3,384]{2,1,0:T(4,128)S(1)}, f32[8,3,384]{2,1,0:T(4,128)}, u32[]{:S(2)}) copy-start(f32[8,3,384]{2,1,0:T(4,128)} %dot_general.197) | copy-start | bytes 110596
  319.5 51.4 %copy-start.99 = (f32[1,8,3]{1,2,0:T(4,128)}, f32[1,8,3]{1,2,0:T(4,128)S(1)}, u32[]{:S(2)}) copy-start(f32[1,8,3]{1,2,0:T(4,128)S(1)} %copy.721) | copy-start | bytes 292
  321.0 7.9 %copy-start.73 = (pred[8]{0:T(512)(128)(4,1)S(1)}, pred[8]{0:T(512)(128)(4,1)}, u32[]{:S(2)}) copy-start(pred[8]{0:T(512)(128)(4,1)} %copy-done.71) | copy-start | bytes 28
  323.1 99.3 %all-gather.16.cloned.1.call-start = ((), (), s32[]{:S(2)}) async-start(), calls=%async_computation.4 | async-start | bytes 1671168 | tf_op jit(solution)/shard_map/all_gather | solution.py:77
  323.3 4.9 collective-permute-start.8
  326.6 5.7 copy-start.79
  326.6 5.0 collective-permute-start.9
  379.4 118.0 %all-gather.18.cloned.1.call-start = ((), (), s32[]{:S(2)}) async-start(), calls=%async_computation.5 | async-start | bytes 1671168 | tf_op jit(solution)/shard_map/all_gather | solution.py:77
  379.5 7.5 %copy-start.74 = (pred[8]{0:T(512)(128)(4,1)S(1)}, pred[8]{0:T(512)(128)(4,1)}, u32[]{:S(2)}) copy-start(pred[8]{0:T(512)(128)(4,1)} %copy-done.71) | copy-start | bytes 28
  379.5 6.2 %collective-permute-start.10 = (f32[3,8,256]{2,1,0:T(8,128)S(1)}, f32[3,8,256]{2,1,0:T(8,128)S(1)}, u32[]{:S(2)}, u32[]{:S(2)}) collective-permute-start(f32[3,8,256]{2,1,0:T(8,128)S(1)} %bitcast.936), channel_id=1, source_target_pairs={{0,16},{16,32},{32,48},{48,64},{64,80},{80,96},{96,112},{1,17},{17... | collective-permute-start | bytes 73736 | tf_op jit(solution)/shard_map/ppermute | solution.py:23
  384.2 8.6 %collective-permute-start.11 = (f32[3,8,256]{2,1,0:T(8,128)}, f32[3,8,256]{2,1,0:T(8,128)}, u32[]{:S(2)}, u32[]{:S(2)}) collective-permute-start(f32[3,8,256]{2,1,0:T(8,128)} %bitcast.754), channel_id=1, source_target_pairs={{16,0},{32,16},{48,32},{64,48},{80,64},{96,80},{112,96},{17,1},{33... | collective-permute-start | bytes 73736 | tf_op jit(solution)/shard_map/ppermute | solution.py:23
  454.2 114.3 %all-gather.20.cloned.1.call-start = ((), (), s32[]{:S(2)}) async-start(), calls=%async_computation.6 | async-start | bytes 1671168 | tf_op jit(solution)/shard_map/all_gather | solution.py:77
  454.3 7.7 %copy-start.75 = (pred[8]{0:T(512)(128)(4,1)S(1)}, pred[8]{0:T(512)(128)(4,1)}, u32[]{:S(2)}) copy-start(pred[8]{0:T(512)(128)(4,1)} %copy-done.71) | copy-start | bytes 28
  454.3 6.4 %collective-permute-start.12 = (f32[3,8,256]{2,1,0:T(8,128)S(1)}, f32[3,8,256]{2,1,0:T(8,128)S(1)}, u32[]{:S(2)}, u32[]{:S(2)}) collective-permute-start(f32[3,8,256]{2,1,0:T(8,128)S(1)} %bitcast.937), channel_id=1, source_target_pairs={{0,16},{16,32},{32,48},{48,64},{64,80},{80,96},{96,112},{1,17},{17... | collective-permute-start | bytes 73736 | tf_op jit(solution)/shard_map/ppermute | solution.py:23
  459.2 8.7 %collective-permute-start.13 = (f32[3,8,256]{2,1,0:T(8,128)}, f32[3,8,256]{2,1,0:T(8,128)}, u32[]{:S(2)}, u32[]{:S(2)}) collective-permute-start(f32[3,8,256]{2,1,0:T(8,128)} %bitcast.752), channel_id=1, source_target_pairs={{16,0},{32,16},{48,32},{64,48},{80,64},{96,80},{112,96},{17,1},{33... | collective-permute-start | bytes 73736 | tf_op jit(solution)/shard_map/ppermute | solution.py:23
  526.1 7.5 %collective-permute-start.14 = (f32[3,8,256]{2,1,0:T(8,128)}, f32[3,8,256]{2,1,0:T(8,128)}, u32[]{:S(2)}, u32[]{:S(2)}) collective-permute-start(f32[3,8,256]{2,1,0:T(8,128)} %bitcast.751), channel_id=1, source_target_pairs={{0,16},{16,32},{32,48},{48,64},{64,80},{80,96},{96,112},{1,17},{17... | collective-permute-start | bytes 73736 | tf_op jit(solution)/shard_map/ppermute | solution.py:23
  528.5 6.5 %collective-permute-start.15 = (f32[3,8,256]{2,1,0:T(8,128)}, f32[3,8,256]{2,1,0:T(8,128)}, u32[]{:S(2)}, u32[]{:S(2)}) collective-permute-start(f32[3,8,256]{2,1,0:T(8,128)} %bitcast.750), channel_id=1, source_target_pairs={{16,0},{32,16},{48,32},{64,48},{80,64},{96,80},{112,96},{17,1},{33... | collective-permute-start | bytes 73736 | tf_op jit(solution)/shard_map/ppermute | solution.py:23
  530.9 5.6 copy-start.76
  531.8 9.1 %copy-start.121 = (pred[8]{0:T(512)(128)(4,1)S(1)}, pred[8]{0:T(512)(128)(4,1)}, u32[]{:S(2)}) copy-start(pred[8]{0:T(512)(128)(4,1)} %copy-done.118) | copy-start | bytes 28
  538.9 7.0 %copy-start.117 = (pred[8]{0:T(512)(128)(4,1)S(1)}, pred[8]{0:T(512)(128)(4,1)}, u32[]{:S(2)}) copy-start(pred[8]{0:T(512)(128)(4,1)} %copy-done.114) | copy-start | bytes 28
  584.4 8.3 %copy-start.104 = (pred[8]{0:T(512)(128)(4,1)S(1)}, pred[8]{0:T(512)(128)(4,1)}, u32[]{:S(2)}) copy-start(pred[8]{0:T(512)(128)(4,1)} %copy-done.102) | copy-start | bytes 28
  584.4 8.3 %copy-start.107 = (pred[8]{0:T(512)(128)(4,1)S(1)}, pred[8]{0:T(512)(128)(4,1)}, u32[]{:S(2)}) copy-start(pred[8]{0:T(512)(128)(4,1)} %copy-done.105) | copy-start | bytes 28
  584.4 8.3 %copy-start.110 = (pred[8]{0:T(512)(128)(4,1)S(1)}, pred[8]{0:T(512)(128)(4,1)}, u32[]{:S(2)}) copy-start(pred[8]{0:T(512)(128)(4,1)} %copy-done.108) | copy-start | bytes 28
  584.4 8.3 %copy-start.113 = (pred[8]{0:T(512)(128)(4,1)S(1)}, pred[8]{0:T(512)(128)(4,1)}, u32[]{:S(2)}) copy-start(pred[8]{0:T(512)(128)(4,1)} %copy-done.111) | copy-start | bytes 28
  (121 other events, 217.3 us)
Sparse Core Ops, SparseCore 0:
  49.8 46.6 all-gather.7
  123.5 42.9 all-gather.9
  221.5 42.9 all-gather.11
  323.3 39.9 all-gather.13
  379.5 42.9 all-gather.15
  454.3 42.9 all-gather.17
  525.5 42.9 all-gather.19
where the time goes:
time: 620 us; the launch traced here: 607 us
  local copies, waits for them, and re-layouts  207 us (33%)
  waiting for transfers between devices  160 us (26%)
  other arithmetic  92.3 us (15%)
  blocking collectives  62.9 us (10%)
  matrix products  41.7 us (7%)
  starting transfers between devices  23.6 us (4%)
  between operations  19.2 us (3%)
    all_gather x7, waiting for transfers between devices, near_faces(): gathered = lax.all_gather(face_rows, 'mem', axis=0, tiled=True)  158 us
    reduce_sum x48, other arithmetic, coarsen(): average = jnp.mean(squares, axis=(-3, -1), keepdims=True)  42 us
    unnamed x1, blocking collectives  38.1 us
    reshape x42, local copies, waits for them, and re-layouts, coarsen(): return jnp.broadcast_to(average, squares.shape).reshape(leading + (FACE,))  35.4 us
    transpose x35, local copies, waits for them, and re-layouts, ghost_set(): ghost_rows[:, direction].transpose(1, 0, 2)  31.4 us
    dot_general x32, matrix products, beside(): jnp.einsum('cbim,lm->cbil', ghosts[direction].reshape(channels, blocks_he...  27.8 us
    all_gather x1, blocking collectives, near_faces(): gathered = lax.all_gather(face_rows, 'mem', axis=0, tiled=True)  24.8 us
    ppermute x16, starting transfers between devices, shifted_2(): return lax.ppermute(block, axis, route)  23.3 us
  transfers between devices with their start and end apart: 23, of which 9 were waited for; matrix products, arithmetic and copies ran while one was open for 20% of the time, Pallas kernels for 0%

commit v1 on v0

v1 whole, which is shorter than its diff:
```python
import functools
import math

import jax
import jax.numpy as jnp
from jax import lax
from jax.experimental import pallas as pl
from jax.experimental.pallas import tpu as pltpu
from jax.sharding import PartitionSpec as P

EDGE = 16
DEG = 3
CELLS = 4096
CAP = 4
B = 8
LANES = 128
ROWS = 8
NC = 384

MASS_TERM = 1.0
LOWER_BOUND = 0.25
UPPER_BOUND = 2.0
MIDPOINT = 0.5 * (UPPER_BOUND + LOWER_BOUND)
HALF_WIDTH = 0.5 * (UPPER_BOUND - LOWER_BOUND)
SIGMA = MIDPOINT / HALF_WIDTH

MESH = pl.DeviceIdType.MESH
F32 = jnp.float32


def plan_kernel(members, owner_ref, block_ref, want_ref, pos_ref, count):
    sub = lax.broadcasted_iota(jnp.int32, (members, 1, LANES), 0)
    lane = lax.broadcasted_iota(jnp.int32, (members, 1, LANES), 2)
    for m in range(members):
        count[m] = 0
    want = jnp.zeros((members, 1, LANES), jnp.int32)
    for row in range(4 * B):
        b, d = row // 4, row % 4
        owner = owner_ref[row, 0]
        slot = count[owner]
        count[owner] = slot + 1
        pos_ref[row] = owner * CAP + slot
        tile = (d ^ 1) * B + block_ref[b, d]
        want = jnp.where((sub == owner) & (lane == slot), tile, want)
    want_ref[...] = want


def main_kernel(
    groups, members,
    forcing, viscosity, refinement, pos, plane, hanging, want, solver,
    x_out, r_out,
    S, E, D, ID, W, WK, WJ, F, FT, SEND, RV0, RV1, RZ0, RZ1, GB, G, RQ, RQS, CV, CR, SV,
    send_sem, recv_sem, zsend_sem, zrecv_sem, rq_send, rq_recv, c_send, c_recv, local_sem,
):
    q = lax.axis_index("grp")
    me = lax.axis_index("mem")
    up = lax.rem(q + 1, groups)
    down = lax.rem(q + groups - 1, groups)
    RV = (RV0, RV1)
    RZ = (RZ0, RZ1)

    lane = lax.broadcasted_iota(jnp.int32, (B, LANES), 1)
    sub = lax.broadcasted_iota(jnp.int32, (B, LANES), 0)
    lane16 = lane % EDGE
    group16 = lane // EDGE
    first_k = lane16 == 0
    last_k = lane16 == EDGE - 1
    first_j = lane < EDGE
    last_j = lane >= LANES - EDGE
    odd_1 = lane % 2 == 1
    odd_16 = group16 % 2 == 1

    def roll(v, shift):
        shift = shift % LANES
        return v if shift == 0 else pltpu.roll(v, shift, 1)

    def member(off):
        return lax.rem(me + off, members)

    barrier = pltpu.get_barrier_semaphore()
    for off in range(1, members):
        pl.semaphore_signal(barrier, inc=1, device_id=(q, member(off)), device_id_type=MESH)
    for other in (up, down):
        pl.semaphore_signal(barrier, inc=1, device_id=(other, me), device_id_type=MESH)
    pl.semaphore_wait(barrier, members + 1)

    def request(target, source, slot):
        return pltpu.make_async_remote_copy(
            src_ref=want.at[target], dst_ref=RQ.at[source],
            send_sem=rq_send.at[target], recv_sem=rq_recv.at[slot],
            device_id=(q, target), device_id_type=MESH)

    for off in range(1, members):
        request(member(off), me, me).start()
    RQ[me] = want[me]

    for t in range(3):
        SV[t * 3 * B:(t + 1) * 3 * B, :] = solver[:, t * LANES:(t + 1) * LANES]
    factor_i = jnp.zeros((B, LANES), jnp.int32)
    for b in range(B):
        factor_i = jnp.where(sub == b, refinement[b], factor_i)
    factor = jnp.exp2(-factor_i.astype(F32))
    for v in range(32):
        E[v] = viscosity[:, v * LANES:(v + 1) * LANES] * factor

    def pack_into(planes, row0):
        zero = jnp.zeros((B, LANES), F32)
        p0, p1, p2, p3 = [zero, zero], [zero, zero], [zero, zero], [zero, zero]
        for i in range(EDGE):
            at = lane16 == i
            ih, il = i // 8, i % 8
            tiles = [planes(i, 0), planes(i, 1)]
            for jh in range(2):
                p0[jh] = jnp.where(at, roll(tiles[jh], i), p0[jh])
                p1[jh] = jnp.where(at, roll(tiles[jh], i - 15), p1[jh])
            here = group16 == il
            p2[ih] = jnp.where(here, roll(tiles[0], il * 16), p2[ih])
            p3[ih] = jnp.where(here, roll(tiles[1], il * 16 - 112), p3[ih])
            if i == 0:
                p4 = tiles
            if i == EDGE - 1:
                p5 = tiles
        for d, face in enumerate((p0, p1, p2, p3, p4, p5)):
            for half in range(2):
                F[pl.ds(d * B * ROWS + row0 + half, B, stride=ROWS), :] = face[half]

    def face_copy(par, rows, target, source, slot):
        return pltpu.make_async_remote_copy(
            src_ref=SEND.at[pl.ds(target * CAP, CAP), pl.ds(0, rows), :],
            dst_ref=RV[par].at[pl.ds(source * CAP, CAP), pl.ds(0, rows), :],
            send_sem=send_sem.at[target], recv_sem=recv_sem.at[par, slot],
            device_id=(q, target), device_id_type=MESH)

    def plane_copy(par, rows, which):
        return pltpu.make_async_remote_copy(
            src_ref=FT.at[pl.ds((5 - which) * B, B), pl.ds(0, rows), :],
            dst_ref=RZ[par].at[pl.ds(which * B, B), pl.ds(0, rows), :],
            send_sem=zsend_sem.at[which], recv_sem=zrecv_sem.at[par, which],
            device_id=((up, down)[which], me), device_id_type=MESH)

    def send_faces(par, rows):
        for tile in range(6 * B):
            FT[tile] = F[tile * ROWS:(tile + 1) * ROWS, :]
        for which in range(2):
            plane_copy(par, rows, which).start()

        def fill(m, carry):
            for s in range(CAP):
                tile = RQS[m, 0, s]
                SEND[m * CAP + s] = FT[tile]
            return carry

        lax.fori_loop(0, members, fill, 0)
        for off in range(1, members):
            face_copy(par, rows, member(off), me, me).start()
        for s in range(CAP):
            RV[par][me * CAP + s] = SEND[me * CAP + s]

    def receive_faces(par, rows):
        for off in range(1, members):
            source = member(off)
            face_copy(par, rows, source, source, source).wait_recv()
        for which in range(2):
            plane_copy(par, rows, which).wait_recv()
        for d in range(4):
            for b in range(B):
                GB[pl.ds((d * B + b) * ROWS, ROWS), :] = RV[par][pos[b * 4 + d]]
        for which in range(2):
            for b in range(B):
                tile = which * B + plane[b, which]
                GB[pl.ds(((4 + which) * B + b) * ROWS, ROWS), :] = RZ[par][tile]
        for d in range(6):
            hang = jnp.broadcast_to(hanging[:, d:d + 1], (B, LANES)) == 1
            for row in range(rows):
                g = GB[pl.ds(d * B * ROWS + row, B, stride=ROWS), :]
                pair = g + jnp.where(odd_1, roll(g, 1), roll(g, -1))
                mean = 0.25 * (pair + jnp.where(odd_16, roll(pair, 16), roll(pair, -16)))
                g = jnp.where(hang, mean, g)
                if d == 4:
                    g = jnp.where(q > 0, g, 0.0)
                if d == 5:
                    g = jnp.where(q < groups - 1, g, 0.0)
                G[d * ROWS + row] = g
        for off in range(1, members):
            target = member(off)
            face_copy(par, rows, target, me, me).wait_send()
        for which in range(2):
            plane_copy(par, rows, which).wait_send()

    def k_ghosts(row0, i, jh):
        lower = roll(G[0 * ROWS + row0 + jh], -i)
        upper = roll(G[1 * ROWS + row0 + jh], 15 - i)
        return lower, upper

    def j_ghost(row0, i, jh):
        ih, il = i // 8, i % 8
        if jh == 0:
            return roll(G[2 * ROWS + row0 + ih], -il * 16)
        return roll(G[3 * ROWS + row0 + ih], 112 - il * 16)

    pack_into(lambda i, jh: E[2 * i + jh], 0)
    for off in range(1, members):
        source = member(off)
        request(source, source, source).wait_recv()
    to_smem = pltpu.make_async_copy(RQ, RQS, local_sem)
    to_smem.start()
    to_smem.wait()
    send_faces(0, 2)
    for off in range(1, members):
        request(member(off), me, me).wait_send()
    receive_faces(0, 2)

    for i in range(EDGE):
        e = [E[2 * i], E[2 * i + 1]]
        before = [roll(e[0], 16), roll(e[1], 16)]
        after = [roll(e[0], -16), roll(e[1], -16)]
        for jh in range(2):
            v = 2 * i + jh
            here = e[jh]
            g_low, g_up = k_ghosts(0, i, jh)
            g_j = j_ghost(0, i, jh)
            w0 = 0.5 * (here + jnp.where(first_k, g_low, roll(here, 1)))
            w1 = 0.5 * (here + jnp.where(last_k, g_up, roll(here, -1)))
            if jh == 0:
                w2 = 0.5 * (here + jnp.where(first_j, g_j, before[0]))
                w3 = 0.5 * (here + jnp.where(last_j, after[1], after[0]))
                W[2, v] = jnp.where(first_j, 0.0, w2)
                W[3, v] = w3
                WJ[v] = jnp.where(first_j, w2, 0.0)
            else:
                w2 = 0.5 * (here + jnp.where(first_j, before[0], before[1]))
                w3 = 0.5 * (here + jnp.where(last_j, g_j, after[1]))
                W[2, v] = w2
                W[3, v] = jnp.where(last_j, 0.0, w3)
                WJ[v] = jnp.where(last_j, w3, 0.0)
            low = E[v - 2] if i > 0 else G[4 * ROWS + jh]
            high = E[v + 2] if i < EDGE - 1 else G[5 * ROWS + jh]
            w4 = 0.5 * (here + low)
            w5 = 0.5 * (here + high)
            W[0, v] = jnp.where(first_k, 0.0, w0)
            W[1, v] = jnp.where(last_k, 0.0, w1)
            WK[v] = jnp.where(first_k, w0, jnp.where(last_k, w1, 0.0))
            W[4, v] = w4
            W[5, v] = w5
            diagonal = MASS_TERM * here + w0 + w1 + w2 + w3 + w4 + w5
            D[v] = diagonal
            ID[v] = 1.0 / diagonal

    def cell(v):
        return slice(v * LANES, (v + 1) * LANES)

    def start_smooth(first):
        def body(c, carry):
            def value(i, jh):
                v = 2 * i + jh
                r = forcing[c, :, cell(v)] if first else r_out[c, :, cell(v)]
                s = r * (ID[v] * (1.0 / MIDPOINT))
                S[c, v] = s
                return s
            pack_into(value, c * 2)
            return carry
        lax.fori_loop(0, 3, body, 0)

    def interior(first):
        def body(c, carry):
            for i in range(EDGE):
                s = [S[c, 2 * i], S[c, 2 * i + 1]]
                before = [roll(s[0], 16), roll(s[1], 16)]
                after = [roll(s[0], -16), roll(s[1], -16)]
                for jh in range(2):
                    v = 2 * i + jh
                    here = s[jh]
                    r = forcing[c, :, cell(v)] if first else r_out[c, :, cell(v)]
                    acc = W[0, v] * roll(here, 1) + W[1, v] * roll(here, -1)
                    if jh == 0:
                        acc += W[2, v] * before[0]
                        acc += W[3, v] * jnp.where(last_j, after[1], after[0])
                    else:
                        acc += W[2, v] * jnp.where(first_j, before[0], before[1])
                        acc += W[3, v] * after[1]
                    if i > 0:
                        acc += W[4, v] * S[c, v - 2]
                    if i < EDGE - 1:
                        acc += W[5, v] * S[c, v + 2]
                    r_out[c, :, cell(v)] = r - D[v] * here + acc
                    x_out[c, :, cell(v)] = here if first else x_out[c, :, cell(v)] + here
            return carry
        lax.fori_loop(0, 3, body, 0)

    def finish(follow):
        def body(c, carry):
            row0 = c * 2

            def value(i, jh):
                v = 2 * i + jh
                g_low, g_up = k_ghosts(row0, i, jh)
                r = r_out[c, :, cell(v)]
                r += WK[v] * jnp.where(first_k, g_low, g_up)
                r += WJ[v] * j_ghost(row0, i, jh)
                if i == 0:
                    r += W[4, v] * G[4 * ROWS + row0 + jh]
                if i == EDGE - 1:
                    r += W[5, v] * G[5 * ROWS + row0 + jh]
                r_out[c, :, cell(v)] = r
                if follow is None:
                    return r
                keep, add = follow
                s = r * (ID[v] * add)
                if keep is not None:
                    s += keep * S[c, v]
                S[c, v] = s
                return s

            if follow is None:
                total = jnp.zeros((B, LANES), F32)
                for v in range(32):
                    total += value(v // 2, v % 2)
                CV[c] = total
            else:
                pack_into(value, row0)
            return carry
        lax.fori_loop(0, 3, body, 0)

    def smooth(first, par, at_end):
        rho = 1.0 / SIGMA
        for step in range(DEG):
            send_faces(par, 6)
            interior(first and step == 0)
            receive_faces(par, 6)
            if step < DEG - 1:
                rho_next = 1.0 / (2.0 * SIGMA - rho)
                finish((rho_next * rho, 2.0 * rho_next / HALF_WIDTH))
                rho = rho_next
            else:
                finish(None)
            par = 1 - par

    start_smooth(True)
    smooth(True, 1, None)

    wide = lax.broadcasted_iota(jnp.int32, (B, NC), 1)
    wide_sub = lax.broadcasted_iota(jnp.int32, (B, NC), 0)
    spread = jnp.zeros((B, NC), F32)
    for c in range(3):
        total = jnp.sum(CV[c], axis=1, keepdims=True) * (1.0 / math.sqrt(CELLS))
        spread = jnp.where(wide == me * (3 * B) + 3 * wide_sub + c, total, spread)
    CR[me] = jnp.sum(spread, axis=0, keepdims=True)

    def coarse_copy(target, source, slot):
        return pltpu.make_async_remote_copy(
            src_ref=CR.at[me], dst_ref=CR.at[source],
            send_sem=c_send.at[target], recv_sem=c_recv.at[slot],
            device_id=(q, target), device_id_type=MESH)

    for off in range(1, members):
        coarse_copy(member(off), me, me).start()
    for off in range(1, members):
        source = member(off)
        coarse_copy(source, source, source).wait_recv()
    vector = CR[0]
    for m in range(1, members):
        vector = vector + CR[m]
    for off in range(1, members):
        coarse_copy(member(off), me, me).wait_send()
    vector = jnp.broadcast_to(vector, (B, NC))
    for c in range(3):
        product = jnp.zeros((B, LANES), F32)
        for t in range(3):
            rows = SV[pl.ds(t * 3 * B + c, B, stride=3), :]
            product += rows * vector[:, t * LANES:(t + 1) * LANES]
        correction = jnp.sum(product, axis=1, keepdims=True)
        lifted = jnp.broadcast_to(correction, (B, LANES))
        for v in range(32):
            S[c, v] = lifted
        for d in range(6):
            for half in range(2):
                F[pl.ds(d * B * ROWS + c * 2 + half, B, stride=ROWS), :] = lifted
    send_faces(0, 6)
    interior(False)
    receive_faces(0, 6)
    finish((None, 1.0 / MIDPOINT))
    smooth(False, 1, None)


def local(
    forcing, viscosity, refinement, face_owner, face_block, plane_block, hanging, coarse_solver
):
    groups, members = lax.axis_size("grp"), lax.axis_size("mem")
    vmem = pl.BlockSpec(memory_space=pltpu.VMEM)
    smem = pl.BlockSpec(memory_space=pltpu.SMEM)
    want, pos = pl.pallas_call(
        functools.partial(plan_kernel, members),
        out_shape=(
            jax.ShapeDtypeStruct((members, 1, LANES), jnp.int32),
            jax.ShapeDtypeStruct((4 * B,), jnp.int32),
        ),
        in_specs=[smem, smem],
        out_specs=(vmem, smem),
        scratch_shapes=[pltpu.SMEM((members,), jnp.int32)],
        name="plan",
    )(face_owner, face_block)

    tiles = 2 * EDGE
    dma = pltpu.SemaphoreType.DMA
    field = jax.ShapeDtypeStruct(forcing.shape, F32)
    return pl.pallas_call(
        functools.partial(main_kernel, groups, members),
        out_shape=(field, field),
        in_specs=[vmem, vmem, smem, smem, smem, vmem, vmem, vmem],
        out_specs=(vmem, vmem),
        scratch_shapes=[
            pltpu.VMEM((3, tiles, B, LANES), F32),
            pltpu.VMEM((tiles, B, LANES), F32),
            pltpu.VMEM((tiles, B, LANES), F32),
            pltpu.VMEM((tiles, B, LANES), F32),
            pltpu.VMEM((6, tiles, B, LANES), F32),
            pltpu.VMEM((tiles, B, LANES), F32),
            pltpu.VMEM((tiles, B, LANES), F32),
            pltpu.VMEM((6 * B * ROWS, LANES), F32),
            pltpu.VMEM((6 * B, ROWS, LANES), F32),
            pltpu.VMEM((members * CAP, ROWS, LANES), F32),
            pltpu.VMEM((members * CAP, ROWS, LANES), F32),
            pltpu.VMEM((members * CAP, ROWS, LANES), F32),
            pltpu.VMEM((2 * B, ROWS, LANES), F32),
            pltpu.VMEM((2 * B, ROWS, LANES), F32),
            pltpu.VMEM((6 * B * ROWS, LANES), F32),
            pltpu.VMEM((6 * ROWS, B, LANES), F32),
            pltpu.VMEM((members, 1, LANES), jnp.int32),
            pltpu.SMEM((members, 1, LANES), jnp.int32),
            pltpu.VMEM((3, B, LANES), F32),
            pltpu.VMEM((members, 1, NC), F32),
            pltpu.VMEM((9 * B, LANES), F32),
            dma((members,)),
            dma((2, members)),
            dma((2,)),
            dma((2, 2)),
            dma((members,)),
            dma((members,)),
            dma((members,)),
            dma((members,)),
            dma,
        ],
        compiler_params=pltpu.CompilerParams(collective_id=0, has_side_effects=True),
        name="vcycle",
    )(forcing, viscosity, refinement, pos, plane_block, hanging, want, coarse_solver[0])


def solution(mesh):
    in_specs = (
        P(None, ("grp", "mem"), None),
        P(("grp", "mem"), None),
        P(("grp", "mem")),
        P(("grp", "mem"), None),
        P(("grp", "mem"), None),
        P(("grp", "mem"), None),
        P(("grp", "mem"), None),
        P("grp", "mem", None),
    )
    out_specs = (P(None, ("grp", "mem"), None), P(None, ("grp", "mem"), None))
    return jax.shard_map(local, mesh=mesh, in_specs=in_specs, out_specs=out_specs, check_vma=False)
```

time: 620 us -> 81.9 us (0.13); the launches traced: 607 us -> 81.6 us
  local copies, waits for them, and re-layouts: 207 us -> 5.29 us
  waiting for transfers between devices: 160 us -> 0 us
  other arithmetic: 92.3 us -> 0 us
  Pallas kernels: 0 us -> 75.6 us
  blocking collectives: 62.9 us -> 0 us
  matrix products: 41.7 us -> 0 us
  starting transfers between devices: 23.6 us -> 0 us
  between operations: 19.2 us -> 0.67 us
    all_gather x7 -> x0, waiting for transfers between devices: 158 us -> none  [near_faces(): gathered = lax.all_gather(face_rows, 'mem', axis=0, tiled=True)]
    pallas_call x0 -> x2, Pallas kernels: none -> 75.6 us  [the longest x1 73.7 us: local(): pl.pallas_call(functools.partial(main_kernel, groups, members), out_shape...]
    reshape x95 -> x0, local copies, waits for them, and re-layouts: 74 us -> none  [the longest x42 35.4 us: coarsen(): return jnp.broadcast_to(average, squares.shape).reshape(leading + (FACE,))]
    reduce_sum x48 -> x0, other arithmetic: 42 us -> none  [coarsen(): average = jnp.mean(squares, axis=(-3, -1), keepdims=True)]
    dot_general x49 -> x0, matrix products: 41.7 us -> none  [the longest x32 27.8 us: beside(): jnp.einsum('cbim,lm->cbil', ghosts[direction].reshape(channels, blocks_he...]
    unnamed x1 -> x0, blocking collectives: 38.1 us -> none
    transpose x43 -> x0, local copies, waits for them, and re-layouts: 37.2 us -> none  [the longest x35 31.4 us: ghost_set(): ghost_rows[:, direction].transpose(1, 0, 2)]
    gather x24 -> x0, local copies, waits for them, and re-layouts: 30.1 us -> none  [the longest x8 16.5 us: near_faces(): return gathered[owners * (4 * blocks_here) + wanted]]
  transfers between devices with their start and end apart: 23 -> 0, of which waited for: 9 -> 0; matrix products, arithmetic and copies ran while one was open for 20% -> 0% of each run, Pallas kernels for 0% -> 0%
where the time goes in v1:
time: 81.9 us; the launch traced here: 81.6 us
  Pallas kernels  75.6 us (92%)
  local copies, waits for them, and re-layouts  5.29 us (6%)
    pallas_call x1, Pallas kernels, local(): pl.pallas_call(functools.partial(main_kernel, groups, members), out_shape...  73.7 us
    unnamed x11, local copies, waits for them, and re-layouts  5.29 us
    pallas_call x1, Pallas kernels, local(): pl.pallas_call(functools.partial(plan_kernel, members), out_shape=(jax.Sh...  1.91 us

profile of v1, /device:TPU:0, one launch (start us, length us, event | category | flops | bytes accessed | tf_op | source)
XLA Modules:
  0.0 81.6 jit_solution(9253574430393520322)
XLA Ops:
  0.6 0.0 copy-start.1
  0.6 1.4 %copy.11.block_ref = s32[8,4]{1,0:T(8,128)} copy(s32[8,4]{0,1:T(4,128)} %param.12) | data formatting | bytes 256 | tf_op args[4]
  2.0 0.0 copy-done.1
  2.0 0.0 copy-start.2
  2.0 0.7 copy.12.plane
  2.7 0.0 copy-done.2
  2.7 0.7 copy.10.owner_ref
  3.4 1.9 %plan.1 = (s32[16,1,128]{2,1,0:T(1,128)}, s32[32]{0:T(128)}) custom-call(s32[32,1]{1,0:T(8,128)} %copy.10.owner_ref, s32[8,4]{1,0:T(8,128)} %copy.11.block_ref), custom_call_target="tpu_custom_call" | custom-call | tf_op jit(solution)/shard_map/plan/pallas_call | solution.py:391
  5.3 73.7 %vcycle.1 = (f32[3,8,4096]{2,1,0:T(8,128)}, f32[3,8,4096]{2,1,0:T(8,128)}) custom-call(f32[3,8,4096]{2,1,0:T(8,128)} %forcing.1, f32[8,4096]{1,0:T(8,128)} %viscosity.1, s32[8]{0:T(128)} %refinement.1, s32[32]{0:T(128)} %get-tuple-element.4.pos, s32[8,2]{1,0:T(8,128)} %copy.12.plane, s32[8,6]{1,0:T(8,128)} %hanging.1, s32[16,1,128]{2,1,0:T(1,128)} %get-tuple-element.5.want, ...), custom_call_target="tpu_custom_call" | custom-call | tf_op jit(solution)/shard_map/vcycle/pallas_call | solution.py:406
  79.0 0.0 copy-start
  79.0 1.8 %copy.15 = f32[3,8,4096]{2,1,0:T(8,128)} copy(f32[3,8,4096]{2,1,0:T(8,128)} %get-tuple-element.8) | data formatting | bytes 786432
  80.9 0.0 copy-done
  80.9 0.7 copy.16
Async XLA Ops:
  0.6 1.4 %copy-start.1 = (s32[8,2]{0,1:T(2,128)S(1)}, s32[8,2]{0,1:T(2,128)}, u32[]{:S(2)}) copy-start(s32[8,2]{0,1:T(2,128)} %param.13) | copy-start | bytes 196
  2.0 0.7 copy-start.2
  79.0 1.8 %copy-start = (f32[3,8,4096]{2,1,0:T(8,128)S(1)}, f32[3,8,4096]{2,1,0:T(8,128)}, u32[]{:S(2)}) copy-start(f32[3,8,4096]{2,1,0:T(8,128)} %get-tuple-element.9) | copy-start | bytes 1179652
